TPU v7x, 32 devices: a whole 2x2x4 slice. The times are simulated.
32 devices in a mesh: row: 8 (over z, x), col: 4 (over y, core).
Axes of the slice: x: 2, y: 2, z: 4, core: 2. Of those that a mesh axis runs over, the one named last changes fastest.
Arguments:
- panel: float32 [8, 16384, 4, 1024], P('row', None, 'col'), may hold values from -1 to 4, as said below
- rhs: float32 [8, 16384, 256], P('row'), may hold values from -6 to 6
Outputs:
- solved: float32 [4, 1024, 256], P('col')
- remainder: float32 [8, 16384, 256], P('row', None, 'col')
Inputs may be any that keep to these rules, and one draw needn't show every extreme that they name: panel is lower triangular in the global indices: entries with column above row are zero, diagonal entries lie between 2 and 4, the others are of size about 1 / sqrt(4096).
All inputs are finite; a program needn't handle non-finite values.
Results may differ from a plain program's by a relative error of at most 0.000084.
Values sent between devices are 32-bit elements; how exact they have to be, the bound alone decides.
A program may use at most 256 MiB of HBM per device.

v0:
```python
import jax
import jax.numpy as jnp
from jax import lax
from jax.sharding import PartitionSpec as P

TB = 512
BASE = 128
CHUNKS = 4
LANES = 128


def dot(left, right, precision=lax.Precision.HIGHEST):
    return jnp.matmul(left, right, precision=precision, preferred_element_type=jnp.float32)


def invert_lower(tile):
    size = tile.shape[0]
    count = size // BASE
    blocks = jnp.stack(
        [tile[i * BASE : (i + 1) * BASE, i * BASE : (i + 1) * BASE] for i in range(count)]
    )
    eye = jnp.eye(BASE, dtype=jnp.float32)
    scale = 1.0 / jnp.sum(blocks * eye, axis=2)
    power = -jnp.tril(blocks * scale[:, :, None], -1)
    inverse = eye + power
    reach = 2
    while reach < BASE:
        power = dot(power, power)
        inverse = inverse + dot(inverse, power)
        reach *= 2
    inverse = inverse * scale[:, None, :]
    parts = [inverse[i] for i in range(count)]
    width = BASE
    while len(parts) > 1:
        merged = []
        for i in range(0, len(parts), 2):
            lo = i * width
            below = tile[lo + width : lo + 2 * width, lo : lo + width]
            corner = -dot(parts[i + 1], dot(below, parts[i]))
            top = jnp.concatenate([parts[i], jnp.zeros_like(corner)], 1)
            merged.append(jnp.concatenate([top, jnp.concatenate([corner, parts[i + 1]], 1)], 0))
        parts = merged
        width *= 2
    return parts[0]


def pack(value, factor):
    rows = value.shape[0] // factor
    return jnp.concatenate([value[i * rows : (i + 1) * rows] for i in range(factor)], 1)


def unpack(value, factor):
    width = value.shape[1] // factor
    return jnp.concatenate([value[:, i * width : (i + 1) * width] for i in range(factor)], 0)


def on_device(panel, rhs):
    col_count = lax.axis_size("col")
    here_row = lax.axis_index("row")
    here_col = lax.axis_index("col")
    local_panel = panel.reshape(panel.shape[1], panel.shape[3])
    right_side = rhs.reshape(rhs.shape[1], rhs.shape[2])
    rows, width = right_side.shape
    tile_cols = local_panel.shape[1] // TB
    steps = tile_cols * col_count
    top = local_panel[:TB]
    diag_col = jnp.minimum(here_row // col_count, tile_cols - 1)
    has_diag = jnp.logical_and(here_row < steps, here_row % col_count == here_col)
    picked = lax.dynamic_slice_in_dim(top, diag_col * TB, TB, 1)
    diag = lax.psum(jnp.where(has_diag, picked, 0.0), "col")
    diag = jnp.where(here_row < steps, diag, jnp.eye(TB, dtype=jnp.float32))
    inverse = invert_lower(diag)
    tile_of = jnp.arange(tile_cols * TB) // TB * col_count + here_col
    coupling = dot(inverse, jnp.where((tile_of < here_row)[None, :], top, 0.0))
    direct = jnp.where(has_diag, dot(inverse, right_side[:TB]), 0.0)
    own = [jnp.zeros((TB, width), jnp.float32) for _ in range(tile_cols)]
    for step in range(steps):
        term = direct
        known = -(-step // col_count)
        if known:
            stacked = own[0] if known == 1 else jnp.concatenate(own[:known], 0)
            term = direct - dot(coupling[:, : known * TB], stacked)
        block = lax.psum(jnp.where(here_row == step, term, 0.0), ("row", "col"))
        place = step // col_count
        own[place] = jnp.where(here_col == step % col_count, block, own[place])
    own_solved = own[0] if tile_cols == 1 else jnp.concatenate(own, 0)
    chips = col_count // 2
    part = width // col_count
    half = width // 2
    factor = max(1, LANES // part)
    chip = here_col // 2
    core = here_col % 2

    def columns(target_core, hop):
        target = lax.rem(chip - 1 - hop + 2 * chips, chips) * 2 + target_core
        return lax.dynamic_slice_in_dim(own_solved, target * part, part, 1)

    order = [columns(1 - core, hop) for hop in range(chips)]
    order += [columns(core, hop) for hop in range(chips)]
    weights = jnp.concatenate(order, 1)
    swap = [(c, c ^ 1) for c in range(col_count)]
    ring = [(c, (c + 2) % col_count) for c in range(col_count)]
    size = rows // CHUNKS
    pieces = []
    for chunk in range(CHUNKS):
        lo = chunk * size
        product = dot(local_panel[lo : lo + size], weights, lax.Precision.HIGH)
        paired = product[:, half:] + lax.ppermute(product[:, :half], "col", swap)
        total = pack(paired[:, :part], factor)
        for hop in range(1, chips):
            total = lax.ppermute(total, "col", ring)
            total = total + pack(paired[:, hop * part : (hop + 1) * part], factor)
        mine = lax.dynamic_slice(right_side, (lo, here_col * part), (size, part))
        pieces.append(mine - unpack(total, factor))
    remainder = jnp.concatenate(pieces, 0)
    return (own_solved[None], remainder[None])


def solution(mesh):
    return jax.shard_map(
        on_device,
        mesh=mesh,
        in_specs=(P("row", None, "col", None), P("row", None, None)),
        out_specs=(P("col", None, None), P("row", None, "col")),
        check_vma=False,
    )
```

profile of v0, /device:TPU:0, one launch (start us, length us, event | category | flops | bytes accessed | tf_op | source)
XLA Modules:
  0.0 1318.2 jit_solution(84741691303237066)
XLA Ops:
  13.4 39.0 %all-reduce.13.cloned.1.call-done = f32[512,512]{1,0:T(8,128)} async-done(((f32[512,512]{1,0:T(8,128)}), f32[512,512]{1,0:T(8,128)}) %all-reduce.13.cloned.1.call-update) | async-done | bytes 1048592 | tf_op jit(solution)/shard_map/psum | solution.py:70
  63.6 5.2 fusion.24
  68.8 124.2 %all-reduce.15.cloned.1.call-done = f32[512,256]{1,0:T(8,128)} async-done(((f32[512,256]{1,0:T(8,128)}), f32[512,256]{1,0:T(8,128)}) %all-reduce.15.cloned.1.call-update) | async-done | bytes 524304 | tf_op jit(solution)/shard_map/psum | solution.py:83
  195.9 131.1 %all-reduce.17.cloned.1.call-done = f32[512,256]{1,0:T(8,128)} async-done(((f32[512,256]{1,0:T(8,128)}), f32[512,256]{1,0:T(8,128)}) %all-reduce.17.cloned.1.call-update) | async-done | bytes 524304 | tf_op jit(solution)/shard_map/psum | solution.py:83
  330.0 130.8 %all-reduce.19.cloned.1.call-done = f32[512,256]{1,0:T(8,128)} async-done(((f32[512,256]{1,0:T(8,128)}), f32[512,256]{1,0:T(8,128)}) %all-reduce.19.cloned.1.call-update) | async-done | bytes 524304 | tf_op jit(solution)/shard_map/psum | solution.py:83
  462.7 131.9 %all-reduce.21.cloned.1.call-done = f32[512,256]{1,0:T(8,128)} async-done(((f32[512,256]{1,0:T(8,128)}), f32[512,256]{1,0:T(8,128)}) %all-reduce.21.cloned.1.call-update) | async-done | bytes 524304 | tf_op jit(solution)/shard_map/psum | solution.py:83
  597.7 130.8 %all-reduce.23.cloned.1.call-done = f32[512,256]{1,0:T(8,128)} async-done(((f32[512,256]{1,0:T(8,128)}), f32[512,256]{1,0:T(8,128)}) %all-reduce.23.cloned.1.call-update) | async-done | bytes 524304 | tf_op jit(solution)/shard_map/psum | solution.py:83
  732.2 130.2 %all-reduce.25.cloned.1.call-done = f32[512,256]{1,0:T(8,128)} async-done(((f32[512,256]{1,0:T(8,128)}), f32[512,256]{1,0:T(8,128)}) %all-reduce.25.cloned.1.call-update) | async-done | bytes 524304 | tf_op jit(solution)/shard_map/psum | solution.py:83
  867.0 11.2 all-reduce.29.cloned.1.call-start
  878.2 44.1 %fusion.95 = (f32[1,4096,1,1024]{3,2,1,0:T(1,128)}, f32[1,4096,1,1024]{3,2,1,0:T(1,128)}, f32[1,4096,1,1024]{3,2,1,0:T(1,128)}, f32[1,4096,1,1024]{3,2,1,0:T(1,128)}) fusion(f32[1,16384,1,1024]{3,2,1,0:T(1,128)} %param.2), kind=kLoop, calls=%fused_computation.173 | loop fusion | bytes 134217728 | tf_op jit(solution)/shard_map/slice | solution.py:107
  922.2 74.2 %all-reduce.27.cloned.1.call-done = f32[512,256]{1,0:T(8,128)} async-done(((f32[512,256]{1,0:T(8,128)}), f32[512,256]{1,0:T(8,128)}) %all-reduce.27.cloned.1.call-update) | async-done | bytes 524304 | tf_op jit(solution)/shard_map/psum | solution.py:83
  1001.0 8.4 constant_dynamic-slice_fusion.3
  1009.4 3.2 copy.8
  1012.5 3.2 copy.9
  1015.7 3.2 copy.10
  1020.4 110.0 %all-reduce.29.cloned.1.call-done = f32[512,256]{1,0:T(8,128)} async-done(((f32[512,256]{1,0:T(8,128)}), f32[512,256]{1,0:T(8,128)}) %all-reduce.29.cloned.1.call-update) | async-done | bytes 524304 | tf_op jit(solution)/shard_map/psum | solution.py:83
  1131.6 19.6 %fusion.12 = f32[4096,256]{0,1:T(8,128)S(1)} fusion(f32[1024,256]{1,0:T(8,128)S(1)} %pad_maximum_fusion.7, f32[1,4096,1,1024]{3,2,1,0:T(1,128)} %get-tuple-element.2), kind=kOutput, calls=%fused_computation.12 | convolution fusion | flops 6442450944 | bytes 22020096 | tf_op jit(solution)/shard_map/dot_general | solution.py:13
  1153.9 14.2 %fusion.15 = f32[4096,256]{0,1:T(8,128)S(1)} fusion(f32[1024,256]{1,0:T(8,128)S(1)} %pad_maximum_fusion.7, f32[1,4096,1,1024]{3,2,1,0:T(1,128)S(1)} %bitcast.106), kind=kOutput, calls=%fused_computation.13 | convolution fusion | flops 6442450944 | bytes 22020096 | tf_op jit(solution)/shard_map/dot_general | solution.py:13
  1171.7 19.4 %fusion.18 = f32[4096,256]{0,1:T(8,128)S(1)} fusion(f32[1024,256]{1,0:T(8,128)S(1)} %pad_maximum_fusion.7, f32[1,4096,1,1024]{3,2,1,0:T(1,128)} %get-tuple-element.5), kind=kOutput, calls=%fused_computation.14 | convolution fusion | flops 6442450944 | bytes 22020096 | tf_op jit(solution)/shard_map/dot_general | solution.py:13
  1194.0 14.3 %fusion.21 = f32[4096,256]{0,1:T(8,128)S(1)} fusion(f32[1024,256]{1,0:T(8,128)S(1)} %pad_maximum_fusion.7, f32[1,4096,1,1024]{3,2,1,0:T(1,128)S(1)} %bitcast.104), kind=kOutput, calls=%fused_computation.15 | convolution fusion | flops 6442450944 | bytes 22020096 | tf_op jit(solution)/shard_map/dot_general | solution.py:13
  1222.2 16.8 %collective-permute-done.1 = f32[2048,128]{0,1:T(8,128)S(1)} collective-permute-done((f32[2048,128]{0,1:T(8,128)S(1)}, f32[2048,128]{0,1:T(8,128)S(1)}, u32[]{:S(2)}, u32[]{:S(2)}) %collective-permute-start.1) | collective-permute-done | bytes 1048608 | tf_op jit(solution)/shard_map/ppermute | solution.py:111
  1239.3 22.3 %collective-permute-done.3 = f32[2048,128]{0,1:T(8,128)S(1)} collective-permute-done((f32[2048,128]{0,1:T(8,128)S(1)}, f32[2048,128]{0,1:T(8,128)S(1)}, u32[]{:S(2)}, u32[]{:S(2)}) %collective-permute-start.3) | collective-permute-done | bytes 1048608 | tf_op jit(solution)/shard_map/ppermute | solution.py:111
  1261.7 22.3 %collective-permute-done.5 = f32[2048,128]{0,1:T(8,128)S(1)} collective-permute-done((f32[2048,128]{0,1:T(8,128)S(1)}, f32[2048,128]{0,1:T(8,128)S(1)}, u32[]{:S(2)}, u32[]{:S(2)}) %collective-permute-start.5) | collective-permute-done | bytes 1048608 | tf_op jit(solution)/shard_map/ppermute | solution.py:111
  1284.2 21.6 %collective-permute-done.7 = f32[2048,128]{0,1:T(8,128)S(1)} collective-permute-done((f32[2048,128]{0,1:T(8,128)S(1)}, f32[2048,128]{0,1:T(8,128)S(1)}, u32[]{:S(2)}, u32[]{:S(2)}) %collective-permute-start.7) | collective-permute-done | bytes 1048608 | tf_op jit(solution)/shard_map/ppermute | solution.py:111
  (155 shorter events, 72.3 us)
Async XLA Ops:
  7.2 45.2 %all-reduce.13.cloned.1.call-start = ((), (), s32[]{:S(2)}) async-start(), calls=%async_computation | async-start | bytes 2097152 | tf_op jit(solution)/shard_map/psum | solution.py:70
  13.2 179.8 %all-reduce.15.cloned.1.call-start = ((), (), s32[]{:S(2)}) async-start(), calls=%async_computation.1 | async-start | bytes 1048576 | tf_op jit(solution)/shard_map/psum | solution.py:83
  63.3 263.7 %all-reduce.17.cloned.1.call-start = ((), (), s32[]{:S(2)}) async-start(), calls=%async_computation.2 | async-start | bytes 1048576 | tf_op jit(solution)/shard_map/psum | solution.py:83
  195.9 264.9 %all-reduce.19.cloned.1.call-start = ((), (), s32[]{:S(2)}) async-start(), calls=%async_computation.3 | async-start | bytes 1048576 | tf_op jit(solution)/shard_map/psum | solution.py:83
  328.1 134.5 %copy-start.7 = (f32[512,256]{1,0:T(8,128)}, f32[512,256]{1,0:T(8,128)S(1)}, u32[]{:S(2)}) copy-start(f32[512,256]{1,0:T(8,128)S(1)} %select_select_fusion) | copy-start | bytes 1572868
  329.9 264.7 %all-reduce.21.cloned.1.call-start = ((), (), s32[]{:S(2)}) async-start(), calls=%async_computation.4 | async-start | bytes 1048576 | tf_op jit(solution)/shard_map/psum | solution.py:83
  462.6 265.8 %all-reduce.23.cloned.1.call-start = ((), (), s32[]{:S(2)}) async-start(), calls=%async_computation.5 | async-start | bytes 1048576 | tf_op jit(solution)/shard_map/psum | solution.py:83
  597.6 264.8 %all-reduce.25.cloned.1.call-start = ((), (), s32[]{:S(2)}) async-start(), calls=%async_computation.6 | async-start | bytes 1048576 | tf_op jit(solution)/shard_map/psum | solution.py:83
  732.2 264.2 %all-reduce.27.cloned.1.call-start = ((), (), s32[]{:S(2)}) async-start(), calls=%async_computation.7 | async-start | bytes 1048576 | tf_op jit(solution)/shard_map/psum | solution.py:83
  867.0 263.4 %all-reduce.29.cloned.1.call-start = ((), (), s32[]{:S(2)}) async-start(), calls=%async_computation.8 | async-start | bytes 1048576 | tf_op jit(solution)/shard_map/psum | solution.py:83
  1018.9 111.5 %copy-start.9 = (f32[512,256]{1,0:T(8,128)S(1)}, f32[512,256]{1,0:T(8,128)}, u32[]{:S(2)}) copy-start(f32[512,256]{1,0:T(8,128)} %copy-done.8) | copy-start | bytes 1572868
  1130.5 23.4 %slice-start.4 = ((s8[16777216]{0:T(1024)(128)(4,1)}), s8[4194304]{0:T(1024)(128)(4,1)S(1)}, s32[]{:S(2)}) async-start(s8[16777216]{0:T(1024)(128)(4,1)} %bitcast.105), calls=%async_computation.13 | async-start | bytes 8388608
  1131.6 22.3 %slice-start.5 = ((s8[16777216]{0:T(1024)(128)(4,1)}), s8[4194304]{0:T(1024)(128)(4,1)S(1)}, s32[]{:S(2)}) async-start(s8[16777216]{0:T(1024)(128)(4,1)} %bitcast.105), calls=%async_computation.14 | async-start | bytes 8388608
  1131.6 22.3 %slice-start.6 = ((s8[16777216]{0:T(1024)(128)(4,1)}), s8[4194304]{0:T(1024)(128)(4,1)S(1)}, s32[]{:S(2)}) async-start(s8[16777216]{0:T(1024)(128)(4,1)} %bitcast.105), calls=%async_computation.15 | async-start | bytes 8388608
  1131.6 22.3 %slice-start.7 = ((s8[16777216]{0:T(1024)(128)(4,1)}), s8[4194304]{0:T(1024)(128)(4,1)S(1)}, s32[]{:S(2)}) async-start(s8[16777216]{0:T(1024)(128)(4,1)} %bitcast.105), calls=%async_computation.16 | async-start | bytes 8388608
  1153.9 56.0 %collective-permute-start = (f32[4096,128]{0,1:T(8,128)}, f32[4096,128]{0,1:T(8,128)}, u32[]{:S(2)}, u32[]{:S(2)}) collective-permute-start(f32[4096,128]{0,1:T(8,128)} %slice.264), channel_id=1, source_target_pairs={{0,1},{1,0},{2,3},{3,2},{4,5},{5,4},{6,7},{7,6},{8,9},{9,8},{10,11... | collective-permute-start | bytes 6291464 | tf_op jit(solution)/shard_map/ppermute | solution.py:108
  1168.1 25.8 %slice-start = ((s8[16777216]{0:T(1024)(128)(4,1)}), s8[4194304]{0:T(1024)(128)(4,1)S(1)}, s32[]{:S(2)}) async-start(s8[16777216]{0:T(1024)(128)(4,1)} %bitcast.103), calls=%async_computation.9 | async-start | bytes 8388608
  1171.2 43.3 %collective-permute-start.2 = (f32[4096,128]{0,1:T(8,128)}, f32[4096,128]{0,1:T(8,128)}, u32[]{:S(2)}, u32[]{:S(2)}) collective-permute-start(f32[4096,128]{0,1:T(8,128)} %slice.272), channel_id=1, source_target_pairs={{0,1},{1,0},{2,3},{3,2},{4,5},{5,4},{6,7},{7,6},{8,9},{9,8},{10,11... | collective-permute-start | bytes 6291464 | tf_op jit(solution)/shard_map/ppermute | solution.py:108
  1193.7 24.8 %collective-permute-start.4 = (f32[4096,128]{0,1:T(8,128)}, f32[4096,128]{0,1:T(8,128)S(1)}, u32[]{:S(2)}, u32[]{:S(2)}) collective-permute-start(f32[4096,128]{0,1:T(8,128)} %slice.280), channel_id=1, source_target_pairs={{0,1},{1,0},{2,3},{3,2},{4,5},{5,4},{6,7},{7,6},{8,9},{9,8},{10,11... | collective-permute-start | bytes 6291464 | tf_op jit(solution)/shard_map/ppermute | solution.py:108
  1208.4 12.6 collective-permute-start.6
  1213.0 26.1 %collective-permute-start.1 = (f32[2048,128]{0,1:T(8,128)S(1)}, f32[2048,128]{0,1:T(8,128)S(1)}, u32[]{:S(2)}, u32[]{:S(2)}) collective-permute-start(f32[2048,128]{0,1:T(8,128)S(1)} %pad_maximum_fusion.8), channel_id=1, source_target_pairs={{0,2},{1,3},{2,0},{3,1},{4,6},{5,7},{6,4},{7,5},{8,10},{9,11},{10,... | collective-permute-start | bytes 3145736 | tf_op jit(solution)/shard_map/ppermute | solution.py:111
  1217.0 44.5 %collective-permute-start.3 = (f32[2048,128]{0,1:T(8,128)S(1)}, f32[2048,128]{0,1:T(8,128)S(1)}, u32[]{:S(2)}, u32[]{:S(2)}) collective-permute-start(f32[2048,128]{0,1:T(8,128)S(1)} %pad_maximum_fusion.9), channel_id=1, source_target_pairs={{0,2},{1,3},{2,0},{3,1},{4,6},{5,7},{6,4},{7,5},{8,10},{9,11},{10,... | collective-permute-start | bytes 3145736 | tf_op jit(solution)/shard_map/ppermute | solution.py:111
  1219.5 64.5 %collective-permute-start.5 = (f32[2048,128]{0,1:T(8,128)S(1)}, f32[2048,128]{0,1:T(8,128)S(1)}, u32[]{:S(2)}, u32[]{:S(2)}) collective-permute-start(f32[2048,128]{0,1:T(8,128)S(1)} %pad_maximum_fusion.10), channel_id=1, source_target_pairs={{0,2},{1,3},{2,0},{3,1},{4,6},{5,7},{6,4},{7,5},{8,10},{9,11},{10,... | collective-permute-start | bytes 3145736 | tf_op jit(solution)/shard_map/ppermute | solution.py:111
  1221.6 84.2 %collective-permute-start.7 = (f32[2048,128]{0,1:T(8,128)S(1)}, f32[2048,128]{0,1:T(8,128)S(1)}, u32[]{:S(2)}, u32[]{:S(2)}) collective-permute-start(f32[2048,128]{0,1:T(8,128)S(1)} %pad_maximum_fusion.11), channel_id=1, source_target_pairs={{0,2},{1,3},{2,0},{3,1},{4,6},{5,7},{6,4},{7,5},{8,10},{9,11},{10,... | collective-permute-start | bytes 3145736 | tf_op jit(solution)/shard_map/ppermute | solution.py:111
  (16 other events, 90.1 us)
Sparse Core Ops, SparseCore 0:
  13.3 38.9 all-reduce.12
  63.4 129.5 all-reduce.14
  198.9 128.0 all-reduce.16
  332.7 128.0 all-reduce.18
  466.5 128.0 all-reduce.20
  600.3 128.0 all-reduce.22
  734.3 128.0 all-reduce.24
  868.3 128.0 all-reduce.26
  1002.3 128.0 all-reduce.28
where the time goes:
time: 1330 us; the launch traced here: 1320 us
  waiting for transfers between devices  1090 us (82%)
  matrix products  97.8 us (7%)
  local copies, waits for them, and re-layouts  83.9 us (6%)
  other arithmetic  18.2 us (1%)
  starting transfers between devices  18 us (1%)
  between operations  15.1 us (1%)
    psum x8, waiting for transfers between devices, on_device(): block = lax.psum(jnp.where(here_row == step, term, 0.0), ('row', 'col'))  963 us
    dot_general x31, matrix products, dot(): jnp.matmul(left, right, precision=precision, preferred_element_type=jnp.f...  97.8 us
    ppermute x4, waiting for transfers between devices, on_device(): total = lax.ppermute(total, 'col', ring)  82.9 us
    slice x1, local copies, waits for them, and re-layouts, on_device(): product = dot(local_panel[lo:lo + size], weights, lax.Precision.HIGH)  44.1 us
    psum x1, waiting for transfers between devices, on_device(): diag = lax.psum(jnp.where(has_diag, picked, 0.0), 'col')  39 us
  transfers between devices with their start and end apart: 17, of which 13 were waited for; matrix products, arithmetic and copies ran while one was open for 10% of the time, Pallas kernels for 0%

commit v1 on v0

--- a/solution.py
+++ b/solution.py
@@ -80,7 +80,9 @@
         if known:
             stacked = own[0] if known == 1 else jnp.concatenate(own[:known], 0)
             term = direct - dot(coupling[:, : known * TB], stacked)
-        block = lax.psum(jnp.where(here_row == step, term, 0.0), ("row", "col"))
+        part_2 = jnp.where(here_row == step, term, 0.0)
+        shards = lax.all_gather(part_2, ("row", "col"), axis=0, tiled=False)
+        block = shards.sum(axis=0)
         place = step // col_count
         own[place] = jnp.where(here_col == step % col_count, block, own[place])
     own_solved = own[0] if tile_cols == 1 else jnp.concatenate(own, 0)

time: 1330 us -> 1250 us (0.940)
  waiting for transfers between devices: 1090 us -> 954 us
  other arithmetic: 18.2 us -> 79.7 us
    psum x8 -> x0, waiting for transfers between devices: 963 us -> none  [on_device(): block = lax.psum(jnp.where(here_row == step, term, 0.0), ('row', 'col'))]
    all_gather x0 -> x8, waiting for transfers between devices: none -> 833 us  [on_device(): shards = lax.all_gather(part_2, ('row', 'col'), axis=0, tiled=False)]
    reduce_sum x0 -> x8, other arithmetic: none -> 59.9 us  [on_device(): block = shards.sum(axis=0)]
where the time goes in v1:
time: 1250 us; the launch traced here: 1240 us
  waiting for transfers between devices  954 us (76%)
  matrix products  96.7 us (8%)
  local copies, waits for them, and re-layouts  84.8 us (7%)
  other arithmetic  79.7 us (6%)
  between operations  14.9 us (1%)
    all_gather x8, waiting for transfers between devices, on_device(): shards = lax.all_gather(part_2, ('row', 'col'), axis=0, tiled=False)  833 us
    dot_general x31, matrix products, dot(): jnp.matmul(left, right, precision=precision, preferred_element_type=jnp.f...  96.7 us
    ppermute x4, waiting for transfers between devices, on_device(): total = lax.ppermute(total, 'col', ring)  81.3 us
    reduce_sum x8, other arithmetic, on_device(): block = shards.sum(axis=0)  59.9 us
    slice x1, local copies, waits for them, and re-layouts, on_device(): product = dot(local_panel[lo:lo + size], weights, lax.Precision.HIGH)  45.1 us
    psum x1, waiting for transfers between devices, on_device(): diag = lax.psum(jnp.where(has_diag, picked, 0.0), 'col')  39 us
  transfers between devices with their start and end apart: 17, of which 13 were waited for; matrix products, arithmetic and copies ran while one was open for 10% of the time, Pallas kernels for 0%

profile of v1, /device:TPU:0, one launch (start us, length us, event | category | flops | bytes accessed | tf_op | source)
XLA Modules:
  0.0 1237.5 jit_solution(14048239833273487301)
XLA Ops:
  13.4 39.0 %all-reduce.5.cloned.1.call-done = f32[512,512]{1,0:T(8,128)} async-done(((f32[512,512]{1,0:T(8,128)}), f32[512,512]{1,0:T(8,128)}) %all-reduce.5.cloned.1.call-update) | async-done | bytes 1048592 | tf_op jit(solution)/shard_map/psum | solution.py:70
  68.8 109.5 %all-gather.17.cloned.1.call-done = f32[16384,256]{1,0:T(8,128)} async-done(((f32[512,256]{1,0:T(8,128)}), f32[16384,256]{1,0:T(8,128)}) %all-gather.17.cloned.1.call-update) | async-done | bytes 16777232 | tf_op jit(solution)/shard_map/all_gather | solution.py:84
  187.1 112.7 %all-gather.19.cloned.1.call-done = f32[16384,256]{1,0:T(8,128)} async-done(((f32[512,256]{1,0:T(8,128)}), f32[16384,256]{1,0:T(8,128)}) %all-gather.19.cloned.1.call-update) | async-done | bytes 16777232 | tf_op jit(solution)/shard_map/all_gather | solution.py:84
  299.7 7.7 reduce_sum.83
  310.4 112.4 %all-gather.21.cloned.1.call-done = f32[16384,256]{1,0:T(8,128)} async-done(((f32[512,256]{1,0:T(8,128)}), f32[16384,256]{1,0:T(8,128)}) %all-gather.21.cloned.1.call-update) | async-done | bytes 16777232 | tf_op jit(solution)/shard_map/all_gather | solution.py:84
  422.8 7.7 reduce_sum.84
  432.6 113.5 %all-gather.23.cloned.1.call-done = f32[16384,256]{1,0:T(8,128)} async-done(((f32[512,256]{1,0:T(8,128)}), f32[16384,256]{1,0:T(8,128)}) %all-gather.23.cloned.1.call-update) | async-done | bytes 16777232 | tf_op jit(solution)/shard_map/all_gather | solution.py:84
  546.1 7.7 reduce_sum.85
  556.8 112.7 %all-gather.25.cloned.1.call-done = f32[16384,256]{1,0:T(8,128)} async-done(((f32[512,256]{1,0:T(8,128)}), f32[16384,256]{1,0:T(8,128)}) %all-gather.25.cloned.1.call-update) | async-done | bytes 16777232 | tf_op jit(solution)/shard_map/all_gather | solution.py:84
  669.5 7.7 reduce_sum.86
  680.9 112.4 %all-gather.27.cloned.1.call-done = f32[16384,256]{1,0:T(8,128)} async-done(((f32[512,256]{1,0:T(8,128)}), f32[16384,256]{1,0:T(8,128)}) %all-gather.27.cloned.1.call-update) | async-done | bytes 16777232 | tf_op jit(solution)/shard_map/all_gather | solution.py:84
  793.4 7.7 reduce_sum.87
  806.0 112.0 %all-gather.29.cloned.1.call-done = f32[16384,256]{1,0:T(8,128)} async-done(((f32[512,256]{1,0:T(8,128)}), f32[16384,256]{1,0:T(8,128)}) %all-gather.29.cloned.1.call-update) | async-done | bytes 16777232 | tf_op jit(solution)/shard_map/all_gather | solution.py:84
  930.3 8.4 constant_dynamic-slice_fusion.3
  949.8 45.1 %fusion.95 = (f32[1,4096,1,1024]{3,2,1,0:T(1,128)}, f32[1,4096,1,1024]{3,2,1,0:T(1,128)}, f32[1,4096,1,1024]{3,2,1,0:T(1,128)}, f32[1,4096,1,1024]{3,2,1,0:T(1,128)}) fusion(f32[1,16384,1,1024]{3,2,1,0:T(1,128)} %param.2), kind=kLoop, calls=%fused_computation.173 | loop fusion | bytes 134217728 | tf_op jit(solution)/shard_map/slice | solution.py:109
  994.9 48.1 %all-gather.31.cloned.1.call-done = f32[16384,256]{1,0:T(8,128)} async-done(((f32[512,256]{1,0:T(8,128)}), f32[16384,256]{1,0:T(8,128)}) %all-gather.31.cloned.1.call-update) | async-done | bytes 16777232 | tf_op jit(solution)/shard_map/all_gather | solution.py:84
  1051.2 19.4 %fusion.12 = f32[4096,256]{0,1:T(8,128)S(1)} fusion(f32[1024,256]{1,0:T(8,128)S(1)} %pad_maximum_fusion.7, f32[1,4096,1,1024]{3,2,1,0:T(1,128)} %get-tuple-element.2), kind=kOutput, calls=%fused_computation.12 | convolution fusion | flops 6442450944 | bytes 22020096 | tf_op jit(solution)/shard_map/dot_general | solution.py:13
  1073.4 14.4 %fusion.15 = f32[4096,256]{0,1:T(8,128)S(1)} fusion(f32[1024,256]{1,0:T(8,128)S(1)} %pad_maximum_fusion.7, f32[1,4096,1,1024]{3,2,1,0:T(1,128)S(1)} %bitcast.114), kind=kOutput, calls=%fused_computation.13 | convolution fusion | flops 6442450944 | bytes 22020096 | tf_op jit(solution)/shard_map/dot_general | solution.py:13
  1091.3 19.3 %fusion.18 = f32[4096,256]{0,1:T(8,128)S(1)} fusion(f32[1024,256]{1,0:T(8,128)S(1)} %pad_maximum_fusion.7, f32[1,4096,1,1024]{3,2,1,0:T(1,128)} %get-tuple-element.5), kind=kOutput, calls=%fused_computation.14 | convolution fusion | flops 6442450944 | bytes 22020096 | tf_op jit(solution)/shard_map/dot_general | solution.py:13
  1113.5 14.2 %fusion.21 = f32[4096,256]{0,1:T(8,128)S(1)} fusion(f32[1024,256]{1,0:T(8,128)S(1)} %pad_maximum_fusion.7, f32[1,4096,1,1024]{3,2,1,0:T(1,128)S(1)} %bitcast.112), kind=kOutput, calls=%fused_computation.15 | convolution fusion | flops 6442450944 | bytes 22020096 | tf_op jit(solution)/shard_map/dot_general | solution.py:13
  1143.4 15.2 %collective-permute-done.1 = f32[2048,128]{0,1:T(8,128)S(1)} collective-permute-done((f32[2048,128]{0,1:T(8,128)S(1)}, f32[2048,128]{0,1:T(8,128)S(1)}, u32[]{:S(2)}, u32[]{:S(2)}) %collective-permute-start.1) | collective-permute-done | bytes 1048608 | tf_op jit(solution)/shard_map/ppermute | solution.py:113
  1158.8 22.3 %collective-permute-done.3 = f32[2048,128]{0,1:T(8,128)S(1)} collective-permute-done((f32[2048,128]{0,1:T(8,128)S(1)}, f32[2048,128]{0,1:T(8,128)S(1)}, u32[]{:S(2)}, u32[]{:S(2)}) %collective-permute-start.3) | collective-permute-done | bytes 1048608 | tf_op jit(solution)/shard_map/ppermute | solution.py:113
  1181.3 22.3 %collective-permute-done.5 = f32[2048,128]{0,1:T(8,128)S(1)} collective-permute-done((f32[2048,128]{0,1:T(8,128)S(1)}, f32[2048,128]{0,1:T(8,128)S(1)}, u32[]{:S(2)}, u32[]{:S(2)}) %collective-permute-start.5) | collective-permute-done | bytes 1048608 | tf_op jit(solution)/shard_map/ppermute | solution.py:113
  1203.8 21.5 %collective-permute-done.7 = f32[2048,128]{0,1:T(8,128)S(1)} collective-permute-done((f32[2048,128]{0,1:T(8,128)S(1)}, f32[2048,128]{0,1:T(8,128)S(1)}, u32[]{:S(2)}, u32[]{:S(2)}) %collective-permute-start.7) | collective-permute-done | bytes 1048608 | tf_op jit(solution)/shard_map/ppermute | solution.py:113
  (165 shorter events, 109.7 us)
Async XLA Ops:
  7.2 45.2 %all-reduce.5.cloned.1.call-start = ((), (), s32[]{:S(2)}) async-start(), calls=%async_computation | async-start | bytes 2097152 | tf_op jit(solution)/shard_map/psum | solution.py:70
  13.2 165.1 %all-gather.17.cloned.1.call-start = ((), (), s32[]{:S(2)}) async-start(), calls=%async_computation.1 | async-start | bytes 17301504 | tf_op jit(solution)/shard_map/all_gather | solution.py:84
  63.3 236.4 %all-gather.19.cloned.1.call-start = ((), (), s32[]{:S(2)}) async-start(), calls=%async_computation.2 | async-start | bytes 17301504 | tf_op jit(solution)/shard_map/all_gather | solution.py:84
  185.2 114.5 %copy-start.10 = (f32[512,256]{1,0:T(8,128)}, f32[512,256]{1,0:T(8,128)S(1)}, u32[]{:S(2)}) copy-start(f32[512,256]{1,0:T(8,128)S(1)} %reduce_sum.82) | copy-start | bytes 1572868
  187.0 235.8 %all-gather.21.cloned.1.call-start = ((), (), s32[]{:S(2)}) async-start(), calls=%async_computation.3 | async-start | bytes 17301504 | tf_op jit(solution)/shard_map/all_gather | solution.py:84
  308.5 122.0 %copy-start.7 = (f32[512,256]{1,0:T(8,128)}, f32[512,256]{1,0:T(8,128)S(1)}, u32[]{:S(2)}) copy-start(f32[512,256]{1,0:T(8,128)S(1)} %select_select_fusion) | copy-start | bytes 1572868
  310.3 235.7 %all-gather.23.cloned.1.call-start = ((), (), s32[]{:S(2)}) async-start(), calls=%async_computation.4 | async-start | bytes 17301504 | tf_op jit(solution)/shard_map/all_gather | solution.py:84
  432.3 237.2 %all-gather.25.cloned.1.call-start = ((), (), s32[]{:S(2)}) async-start(), calls=%async_computation.5 | async-start | bytes 17301504 | tf_op jit(solution)/shard_map/all_gather | solution.py:84
  556.7 236.6 %all-gather.27.cloned.1.call-start = ((), (), s32[]{:S(2)}) async-start(), calls=%async_computation.6 | async-start | bytes 17301504 | tf_op jit(solution)/shard_map/all_gather | solution.py:84
  680.9 237.2 %all-gather.29.cloned.1.call-start = ((), (), s32[]{:S(2)}) async-start(), calls=%async_computation.7 | async-start | bytes 17301504 | tf_op jit(solution)/shard_map/all_gather | solution.py:84
  805.6 237.4 %all-gather.31.cloned.1.call-start = ((), (), s32[]{:S(2)}) async-start(), calls=%async_computation.8 | async-start | bytes 17301504 | tf_op jit(solution)/shard_map/all_gather | solution.py:84
  1050.0 23.4 %slice-start.4 = ((s8[16777216]{0:T(1024)(128)(4,1)}), s8[4194304]{0:T(1024)(128)(4,1)S(1)}, s32[]{:S(2)}) async-start(s8[16777216]{0:T(1024)(128)(4,1)} %bitcast.113), calls=%async_computation.13 | async-start | bytes 8388608
  1051.1 22.3 %slice-start.5 = ((s8[16777216]{0:T(1024)(128)(4,1)}), s8[4194304]{0:T(1024)(128)(4,1)S(1)}, s32[]{:S(2)}) async-start(s8[16777216]{0:T(1024)(128)(4,1)} %bitcast.113), calls=%async_computation.14 | async-start | bytes 8388608
  1051.1 22.3 %slice-start.6 = ((s8[16777216]{0:T(1024)(128)(4,1)}), s8[4194304]{0:T(1024)(128)(4,1)S(1)}, s32[]{:S(2)}) async-start(s8[16777216]{0:T(1024)(128)(4,1)} %bitcast.113), calls=%async_computation.15 | async-start | bytes 8388608
  1051.2 22.3 %slice-start.7 = ((s8[16777216]{0:T(1024)(128)(4,1)}), s8[4194304]{0:T(1024)(128)(4,1)S(1)}, s32[]{:S(2)}) async-start(s8[16777216]{0:T(1024)(128)(4,1)} %bitcast.113), calls=%async_computation.16 | async-start | bytes 8388608
  1073.2 56.1 %collective-permute-start = (f32[4096,128]{0,1:T(8,128)}, f32[4096,128]{0,1:T(8,128)}, u32[]{:S(2)}, u32[]{:S(2)}) collective-permute-start(f32[4096,128]{0,1:T(8,128)} %slice.264), channel_id=1, source_target_pairs={{0,1},{1,0},{2,3},{3,2},{4,5},{5,4},{6,7},{7,6},{8,9},{9,8},{10,11... | collective-permute-start | bytes 6291464 | tf_op jit(solution)/shard_map/ppermute | solution.py:110
  1087.9 25.6 %slice-start = ((s8[16777216]{0:T(1024)(128)(4,1)}), s8[4194304]{0:T(1024)(128)(4,1)S(1)}, s32[]{:S(2)}) async-start(s8[16777216]{0:T(1024)(128)(4,1)} %bitcast.111), calls=%async_computation.9 | async-start | bytes 8388608
  1091.0 43.0 %collective-permute-start.2 = (f32[4096,128]{0,1:T(8,128)}, f32[4096,128]{0,1:T(8,128)}, u32[]{:S(2)}, u32[]{:S(2)}) collective-permute-start(f32[4096,128]{0,1:T(8,128)} %slice.272), channel_id=1, source_target_pairs={{0,1},{1,0},{2,3},{3,2},{4,5},{5,4},{6,7},{7,6},{8,9},{9,8},{10,11... | collective-permute-start | bytes 6291464 | tf_op jit(solution)/shard_map/ppermute | solution.py:110
  1113.2 24.9 %collective-permute-start.4 = (f32[4096,128]{0,1:T(8,128)}, f32[4096,128]{0,1:T(8,128)}, u32[]{:S(2)}, u32[]{:S(2)}) collective-permute-start(f32[4096,128]{0,1:T(8,128)} %slice.280), channel_id=1, source_target_pairs={{0,1},{1,0},{2,3},{3,2},{4,5},{5,4},{6,7},{7,6},{8,9},{9,8},{10,11... | collective-permute-start | bytes 6291464 | tf_op jit(solution)/shard_map/ppermute | solution.py:110
  1127.9 14.2 %collective-permute-start.6 = (f32[4096,128]{0,1:T(8,128)S(1)}, f32[4096,128]{0,1:T(8,128)S(1)}, u32[]{:S(2)}, u32[]{:S(2)}) collective-permute-start(f32[4096,128]{0,1:T(8,128)S(1)} %slice.288), channel_id=1, source_target_pairs={{0,1},{1,0},{2,3},{3,2},{4,5},{5,4},{6,7},{7,6},{8,9},{9,8},{10,11... | collective-permute-start | bytes 6291464 | tf_op jit(solution)/shard_map/ppermute | solution.py:110
  1132.5 26.1 %collective-permute-start.1 = (f32[2048,128]{0,1:T(8,128)S(1)}, f32[2048,128]{0,1:T(8,128)S(1)}, u32[]{:S(2)}, u32[]{:S(2)}) collective-permute-start(f32[2048,128]{0,1:T(8,128)S(1)} %pad_maximum_fusion.8), channel_id=1, source_target_pairs={{0,2},{1,3},{2,0},{3,1},{4,6},{5,7},{6,4},{7,5},{8,10},{9,11},{10,... | collective-permute-start | bytes 3145736 | tf_op jit(solution)/shard_map/ppermute | solution.py:113
  1136.6 44.5 %collective-permute-start.3 = (f32[2048,128]{0,1:T(8,128)S(1)}, f32[2048,128]{0,1:T(8,128)S(1)}, u32[]{:S(2)}, u32[]{:S(2)}) collective-permute-start(f32[2048,128]{0,1:T(8,128)S(1)} %pad_maximum_fusion.9), channel_id=1, source_target_pairs={{0,2},{1,3},{2,0},{3,1},{4,6},{5,7},{6,4},{7,5},{8,10},{9,11},{10,... | collective-permute-start | bytes 3145736 | tf_op jit(solution)/shard_map/ppermute | solution.py:113
  1140.6 62.9 %collective-permute-start.5 = (f32[2048,128]{0,1:T(8,128)S(1)}, f32[2048,128]{0,1:T(8,128)S(1)}, u32[]{:S(2)}, u32[]{:S(2)}) collective-permute-start(f32[2048,128]{0,1:T(8,128)S(1)} %pad_maximum_fusion.10), channel_id=1, source_target_pairs={{0,2},{1,3},{2,0},{3,1},{4,6},{5,7},{6,4},{7,5},{8,10},{9,11},{10,... | collective-permute-start | bytes 3145736 | tf_op jit(solution)/shard_map/ppermute | solution.py:113
  1142.7 82.6 %collective-permute-start.7 = (f32[2048,128]{0,1:T(8,128)S(1)}, f32[2048,128]{0,1:T(8,128)S(1)}, u32[]{:S(2)}, u32[]{:S(2)}) collective-permute-start(f32[2048,128]{0,1:T(8,128)S(1)} %pad_maximum_fusion.11), channel_id=1, source_target_pairs={{0,2},{1,3},{2,0},{3,1},{4,6},{5,7},{6,4},{7,5},{8,10},{9,11},{10,... | collective-permute-start | bytes 3145736 | tf_op jit(solution)/shard_map/ppermute | solution.py:113
  (17 other events, 97.0 us)
Sparse Core Ops, SparseCore 0:
  13.3 38.9 all-reduce.4
  63.4 114.7 all-gather.16
  187.1 112.5 all-gather.18
  310.4 112.3 all-gather.20
  432.4 113.5 all-gather.22
  556.8 112.5 all-gather.24
  681.0 112.3 all-gather.26
  805.7 112.3 all-gather.28
  930.4 112.5 all-gather.30
